TPU v7x, 128 devices: a whole 4x4x4 slice. The times are simulated.
128 devices in a mesh: req: 16 (over y, x_hi, core), tp: 8 (over x_lo, z).
Axes of the slice: x: 4 (x_hi: 2, x_lo: 2; x = x_hi * 2 + x_lo), y: 4, z: 4, core: 2. Of those that a mesh axis runs over, the one named last changes fastest.
Arguments:
- hidden_in: bfloat16 [16384, 7168], P(('req', 'tp')), may hold values from -6 to 6
- ln_gain: float32 [7168], replicated, may hold values from 0.1 to 1.9
- ln_bias: float32 [7168], replicated, may hold values from -3 to 3
- w_query: bfloat16 [7168, 4096], P(None, 'tp'), may hold values from -0.0625 to 0.0625
- w_key: bfloat16 [7168, 4096], P(None, 'tp'), may hold values from -0.0625 to 0.0625
- w_value: bfloat16 [7168, 4096], P(None, 'tp'), may hold values from -0.0625 to 0.0625
- qkv_bias: float32 [3, 4096], P(None, 'tp'), may hold values from -34 to 34
- segment_ids: int32 [16384], P('req'), may hold values from -1 to 19, as said below
- page_table: int32 [1024], P('req'), may hold values from 0 to 1023, as said below
Outputs:
- context: bfloat16 [16384, 4096], P('req', 'tp')
- kv_cache: bfloat16 [2, 32, 1024, 16, 128], P(None, 'tp', 'req')
Inputs may be any that keep to these rules, and one draw needn't show every extreme that they name: `segment_ids`: within each block of 1024 positions, live positions come first and padding (-1) fills the tail; ids count the block's requests from 0 upward, each request contiguous and starting at a multiple of 32 positions within its block. In every draw one block holds a single request of exactly 1024 positions; every other request has at most 256 positions. `page_table`: every slot is named once. Of the 64 pages of one block of 1024 positions, exactly 4 name slots s with s // 64 equal to each given value.
All inputs are finite; a program needn't handle non-finite values.
Results may differ from a plain program's by a relative error of at most 0.012.
The roundings to bfloat16 on the way count: a program that leaves them out, or rounds other values in their place, can miss the bound.
Values may be sent and summed in bfloat16 or wider, within the bound.
A program may use at most 128 MiB of HBM per device.

v0:
```python
import jax
import jax.numpy as jnp
from jax import lax
from jax.sharding import PartitionSpec as P

HEAD_DIM = 128


def layer_norm(rows, gain, shift):
    values = rows.astype(jnp.float32)
    center = values - jnp.mean(values, axis=1, keepdims=True)
    spread = jnp.mean(center * center, axis=1, keepdims=True)
    return (center * lax.rsqrt(spread + 1e-05) * gain + shift).astype(jnp.bfloat16)


def project(normed, w_query, w_key, w_value, qkv_bias, live):
    query = (
        jnp.dot(normed, w_query, preferred_element_type=jnp.float32) + qkv_bias[0]
    ) * HEAD_DIM ** (-0.5)
    keys = jnp.where(
        live[:, None], jnp.dot(normed, w_key, preferred_element_type=jnp.float32) + qkv_bias[1], 0.0
    )
    values = jnp.where(
        live[:, None],
        jnp.dot(normed, w_value, preferred_element_type=jnp.float32) + qkv_bias[2],
        0.0,
    )
    return jnp.stack([query, keys, values]).astype(jnp.bfloat16)


def head_rows(query_head, key_head, value_head, segments, first, last):
    count = key_head.shape[0]
    query_pos = jnp.arange(first, last)
    key_pos = jnp.arange(0, count)
    visible = (
        (segments[:, None] == segments[None, :])
        & (segments[None, :] >= 0)
        & (key_pos[None, :] <= query_pos[:, None])
    )
    scores = jnp.dot(query_head, key_head.T, preferred_element_type=jnp.float32)
    scores = jnp.where(visible, scores, -1e30)
    top = jnp.max(scores, axis=1, keepdims=True)
    weights = jnp.where(visible, jnp.exp(scores - top), 0.0)
    total = jnp.maximum(jnp.sum(weights, axis=1, keepdims=True), 1.0)
    probs = (weights / total).astype(jnp.bfloat16)
    return jnp.dot(probs, value_head, preferred_element_type=jnp.float32).astype(jnp.bfloat16)


def attend(query, keys, values, segments):
    positions, width = query.shape
    heads = width // HEAD_DIM

    def split(array):
        return array.reshape(positions, heads, HEAD_DIM).transpose(1, 0, 2)

    query_heads, key_heads, value_heads = (split(query), split(keys), split(values))
    attended = lax.map(
        lambda items: head_rows(items[0], items[1], items[2], segments, 0, positions),
        (query_heads, key_heads, value_heads),
    )
    return attended.transpose(1, 0, 2).reshape(positions, width)


def send_pages(keys, values, page_table):
    pages = page_table.shape[0]
    positions, width = keys.shape
    page_rows = positions // pages
    heads = width // HEAD_DIM
    stacked = (
        jnp.stack([keys, values], axis=0)
        .reshape(2, pages, page_rows, heads, HEAD_DIM)
        .transpose(1, 0, 2, 3, 4)
    )
    target = page_table // pages
    local_slot = page_table % pages
    order = jnp.argsort(target, stable=True)
    moved, slots = (
        lax.all_to_all(stacked[order], "req", split_axis=0, concat_axis=0, tiled=True),
        lax.all_to_all(local_slot[order], "req", split_axis=0, concat_axis=0, tiled=True),
    )
    placed = moved[jnp.argsort(slots)]
    return placed.transpose(1, 3, 0, 2, 4)


def on_device(
    hidden_in, ln_gain, ln_bias, w_query, w_key, w_value, qkv_bias, segment_ids, page_table
):
    projected = project(
        layer_norm(lax.all_gather(hidden_in, "tp", axis=0, tiled=True), ln_gain, ln_bias),
        w_query,
        w_key,
        w_value,
        qkv_bias,
        segment_ids >= 0,
    )
    query, keys, values = (projected[0], projected[1], projected[2])
    context = attend(query, keys, values, segment_ids)
    kv_cache = send_pages(keys, values, page_table)
    return (context, kv_cache)


def solution(mesh):
    return jax.shard_map(
        on_device,
        mesh=mesh,
        in_specs=(
            P(("req", "tp"), None),
            P(),
            P(),
            P(None, "tp"),
            P(None, "tp"),
            P(None, "tp"),
            P(None, "tp"),
            P("req"),
            P("req"),
        ),
        out_specs=(P("req", "tp"), P(None, "tp", "req", None, None)),
        check_vma=False,
    )
```

profile of v0, /device:TPU:1, one launch (start us, length us, event | category | flops | bytes accessed | tf_op | source)
XLA Modules:
  0.0 302.4 jit_solution(12135118569450937737)
XLA Ops:
  12.1 8.4 %all-to-all-start.1 = ((s32[16,4,1]{1,2,0:T(1,128)}), s32[16,4,1]{1,2,0:T(1,128)S(1)}, u32[]{:S(2)}, u32[]{:S(2)}) async-start(s32[16,4,1]{1,2,0:T(1,128)} %bitcast.17), calls=%async_computation.1 | async-start | bytes 16384 | tf_op jit(solution)/shard_map/all_to_all | solution.py:79
  22.0 5.4 %all-to-all-done.1 = s32[16,4,1]{1,2,0:T(1,128)S(1)} async-done(((s32[16,4,1]{1,2,0:T(1,128)}), s32[16,4,1]{1,2,0:T(1,128)S(1)}, u32[]{:S(2)}, u32[]{:S(2)}) %all-to-all-start.1) | async-done | bytes 288 | tf_op jit(solution)/shard_map/all_to_all | solution.py:79
  30.8 132.9 %all-gather.2.cloned.1.call-done = bf16[1024,7168]{1,0:T(8,128)(2,1)} async-done(((bf16[128,7168]{1,0:T(8,128)(2,1)}), bf16[1024,7168]{1,0:T(8,128)(2,1)}) %all-gather.2.cloned.1.call-update) | async-done | bytes 14680080 | tf_op jit(solution)/shard_map/all_gather | solution.py:89
  163.7 7.5 %convert_reduce_fusion = f32[1024]{0:T(1024)S(1)} fusion(bf16[1024,7168]{1,0:T(8,128)(2,1)} %all-gather.2.cloned.1.call-done), kind=kLoop, calls=%fused_computation.25 | loop fusion | flops 14679040 | bytes 14684160 | tf_op jit(solution)/shard_map/reduce_sum | solution.py:11
  171.3 9.1 %fusion.17 = f32[1024]{0:T(1024)S(1)} fusion(bf16[1024,7168]{1,0:T(8,128)(2,1)} %all-gather.2.cloned.1.call-done, f32[1024]{0:T(1024)S(1)} %broadcast_multiply_fusion), kind=kLoop, calls=%fused_computation.28 | loop fusion | flops 29359104 | bytes 14688256 | tf_op jit(solution)/shard_map/reduce_sum | solution.py:12
  180.4 15.6 %fusion.20 = bf16[1024,7168]{1,0:T(8,128)(2,1)} fusion(bf16[1024,7168]{1,0:T(8,128)(2,1)} %all-gather.2.cloned.1.call-done, f32[7168]{0:T(1024)S(1)} %copy-done.3, f32[7168]{0:T(1024)S(1)} %copy-done.4, f32[1024]{0:T(1024)S(1)} %add_rsqrt_fusion, f32[1024]{0:T(1024)S(1)} %broadcast_multiply_fusion), kind=kLoop, calls=%fused_computation.31 | loop fusion | flops 44040192 | bytes 29425664 | tf_op jit(solution)/shard_map/convert_element_type | solution.py:13
  196.0 13.2 %select_convert_fusion = bf16[1024,512]{0,1:T(8,128)(2,1)S(1)} fusion(bf16[1024,7168]{1,0:T(8,128)(2,1)} %fusion.20, bf16[7168,512]{1,0:T(8,128)(2,1)} %param.16, f32[512]{0:T(512)S(1)} %bitcast.66, pred[1024]{0:T(1024)(128)(4,1)S(1)} %broadcast_compare_fusion.1), kind=kOutput, calls=%fused_computation.34 | convolution fusion | flops 7517765632 | bytes 23071744 | tf_op jit(solution)/shard_map/dot_general | solution.py:25
  210.5 13.2 %select_convert_fusion.1 = bf16[1024,512]{0,1:T(8,128)(2,1)S(1)} fusion(bf16[1024,7168]{1,0:T(8,128)(2,1)} %fusion.20, bf16[7168,512]{1,0:T(8,128)(2,1)} %param.15, f32[512]{0:T(512)S(1)} %bitcast.65, pred[1024]{0:T(1024)(128)(4,1)S(1)} %broadcast_compare_fusion.1), kind=kOutput, calls=%fused_computation.35 | convolution fusion | flops 7517765632 | bytes 23071744 | tf_op jit(solution)/shard_map/dot_general | solution.py:21
  225.1 13.2 %multiply_convert_fusion = bf16[1024,512]{0,1:T(8,128)(2,1)S(1)} fusion(bf16[1024,7168]{1,0:T(8,128)(2,1)} %fusion.20, bf16[7168,512]{1,0:T(8,128)(2,1)} %param.14, f32[512]{0:T(512)S(1)} %bitcast.64), kind=kOutput, calls=%fused_computation.36 | convolution fusion | flops 7517765632 | bytes 23070720 | tf_op jit(solution)/shard_map/dot_general | solution.py:18
  241.0 2.6 copy.26
  243.6 4.0 %reshape.42 = bf16[2,64,16,4,128]{4,3,2,1,0:T(4,128)(2,1)} reshape(bf16[2,1024,512]{2,1,0:T(8,128)(2,1)} %copy.26) | data formatting | bytes 4194304 | tf_op jit(solution)/shard_map/reshape | solution.py:71
  247.6 2.2 copy.33
  252.0 7.3 %all-to-all-start = ((bf16[64,2,16,4,128]{4,2,3,1,0:T(8,128)(2,1)}), bf16[64,2,16,4,128]{4,2,3,1,0:T(8,128)(2,1)S(1)}, u32[]{:S(2)}, u32[]{:S(2)}) async-start(bf16[64,2,16,4,128]{4,2,3,1,0:T(8,128)(2,1)} %gather_fusion), calls=%async_computation | async-start | bytes 4194304 | tf_op jit(solution)/shard_map/all_to_all | solution.py:78
  259.3 29.7 %while.10 = (s32[]{:T(128)}, bf16[4,1024,128]{2,1,0:T(8,128)(2,1)S(1)}, s32[1024]{0:T(1024)S(1)}, bf16[4,1024,128]{2,1,0:T(8,128)(2,1)}, bf16[4,1024,128]{2,1,0:...) while((s32[]{:T(128)}, bf16[4,1024,128]{2,1,0:T(8,128)(2,1)S(1)}, s32[1024]{0:T(1024)S(1)}, ...), condition=%wide.region_5.6_spmd, body=%wide.region_2.5_spmd.sunk | while | flops 559022080 | bytes 13690957 | solution.py:57
  259.3 2.9 fusion.35
  264.3 2.4 fusion.37
  266.7 2.9 fusion.35
  271.8 2.4 fusion.37
  274.2 2.9 fusion.35
  279.2 2.4 fusion.37
  281.6 2.9 fusion.35
  286.6 2.4 fusion.37
  290.1 2.2 gather_fusion.2
  292.3 3.3 %copy.29 = bf16[2,4,64,16,128]{4,3,2,1,0:T(8,128)(2,1)} copy(bf16[2,4,64,16,128]{4,3,1,0,2:T(8,128)(2,1)} %bitcast.55) | data formatting | bytes 4194304
  (50 shorter events, 26.6 us)
Async XLA Ops:
  7.2 156.6 %all-gather.2.cloned.1.call-start = ((), (), s32[]{:S(2)}) async-start(), calls=%async_computation.2 | async-start | bytes 16515072 | tf_op jit(solution)/shard_map/all_gather | solution.py:89
  12.1 15.4 %all-to-all-start.1 = ((s32[16,4,1]{1,2,0:T(1,128)}), s32[16,4,1]{1,2,0:T(1,128)S(1)}, u32[]{:S(2)}, u32[]{:S(2)}) async-start(s32[16,4,1]{1,2,0:T(1,128)} %bitcast.17), calls=%async_computation.1 | async-start | bytes 16384 | tf_op jit(solution)/shard_map/all_to_all | solution.py:79
  171.2 9.1 %copy-start.3 = (f32[7168]{0:T(1024)S(1)}, f32[7168]{0:T(1024)}, u32[]{:S(2)}) copy-start(f32[7168]{0:T(1024)} %param.13) | copy-start | bytes 86020
  171.3 9.1 %copy-start.4 = (f32[7168]{0:T(1024)S(1)}, f32[7168]{0:T(1024)}, u32[]{:S(2)}) copy-start(f32[7168]{0:T(1024)} %param.12) | copy-start | bytes 86020
  223.7 14.6 %copy-start = (bf16[1024,512]{0,1:T(8,128)(2,1)}, bf16[1024,512]{0,1:T(8,128)(2,1)S(1)}, u32[]{:S(2)}) copy-start(bf16[1024,512]{0,1:T(8,128)(2,1)S(1)} %select_convert_fusion.1) | copy-start | bytes 3145732
  249.8 9.5 %copy-start.1 = (s32[1024]{0:T(1024)S(1)}, s32[1024]{0:T(1024)}, u32[]{:S(2)}) copy-start(s32[1024]{0:T(1024)} %param.18) | copy-start | bytes 12292
  249.8 9.5 %copy-start.2 = (bf16[4,1024,128]{2,1,0:T(8,128)(2,1)S(1)}, bf16[4,1024,128]{2,1,0:T(8,128)(2,1)}, u32[]{:S(2)}) copy-start(bf16[4,1024,128]{2,1,0:T(8,128)(2,1)} %custom-call.6) | copy-start | bytes 3145732
  252.0 38.1 %all-to-all-start = ((bf16[64,2,16,4,128]{4,2,3,1,0:T(8,128)(2,1)}), bf16[64,2,16,4,128]{4,2,3,1,0:T(8,128)(2,1)S(1)}, u32[]{:S(2)}, u32[]{:S(2)}) async-start(bf16[64,2,16,4,128]{4,2,3,1,0:T(8,128)(2,1)} %gather_fusion), calls=%async_computation | async-start | bytes 4194304 | tf_op jit(solution)/shard_map/all_to_all | solution.py:78
Sparse Core Ops, SparseCore 0:
  9.6 154.0 all-gather.1
where the time goes:
time: 303 us; the launch traced here: 302 us
  waiting for transfers between devices  139 us (46%)
  matrix products  60.8 us (20%)
  other arithmetic  48 us (16%)
  local copies, waits for them, and re-layouts  24.3 us (8%)
  starting transfers between devices  15.8 us (5%)
  between operations  14.2 us (5%)
    all_gather x1, waiting for transfers between devices, on_device(): lax.all_gather(hidden_in, 'tp', axis=0, tiled=True)  133 us
    convert_element_type x1, other arithmetic, layer_norm(): (center * lax.rsqrt(spread + 1e-05) * gain + shift).astype(jnp.bfloat16)  15.6 us
    dot_general x1, matrix products, project(): jnp.dot(normed, w_value, preferred_element_type=jnp.float32) + qkv_bias[2]  13.2 us
    dot_general x1, matrix products, project(): jnp.dot(normed, w_query, preferred_element_type=jnp.float32) + qkv_bias[0]  13.2 us
    dot_general x1, matrix products, project(): jnp.dot(normed, w_key, preferred_element_type=jnp.float32) + qkv_bias[1]  13.2 us
    dot_general x4, matrix products, head_rows(): scores = jnp.dot(query_head, key_head.T, preferred_element_type=jnp.float32)  11.7 us
    dot_general x4, matrix products, head_rows(): jnp.dot(probs, value_head, preferred_element_type=jnp.float32)  9.52 us
    reduce_sum x1, other arithmetic, layer_norm(): spread = jnp.mean(center * center, axis=1, keepdims=True)  9.1 us
  transfers between devices with their start and end apart: 3, of which 2 were waited for; matrix products, arithmetic and copies ran while one was open for 13% of the time, Pallas kernels for 0%

commit v1 on v0

--- a/solution.py
+++ b/solution.py
@@ -4,6 +4,7 @@
 from jax.sharding import PartitionSpec as P
 
 HEAD_DIM = 128
+CHUNKS = 4
 
 
 def layer_norm(rows, gain, shift):
@@ -11,21 +12,6 @@
     center = values - jnp.mean(values, axis=1, keepdims=True)
     spread = jnp.mean(center * center, axis=1, keepdims=True)
     return (center * lax.rsqrt(spread + 1e-05) * gain + shift).astype(jnp.bfloat16)
-
-
-def project(normed, w_query, w_key, w_value, qkv_bias, live):
-    query = (
-        jnp.dot(normed, w_query, preferred_element_type=jnp.float32) + qkv_bias[0]
-    ) * HEAD_DIM ** (-0.5)
-    keys = jnp.where(
-        live[:, None], jnp.dot(normed, w_key, preferred_element_type=jnp.float32) + qkv_bias[1], 0.0
-    )
-    values = jnp.where(
-        live[:, None],
-        jnp.dot(normed, w_value, preferred_element_type=jnp.float32) + qkv_bias[2],
-        0.0,
-    )
-    return jnp.stack([query, keys, values]).astype(jnp.bfloat16)
 
 
 def head_rows(query_head, key_head, value_head, segments, first, last):
@@ -82,18 +68,34 @@
     return placed.transpose(1, 3, 0, 2, 4)
 
 
+def project_chunks(normed_local, w_query, w_key, w_value, qkv_bias, live, chunks):
+    width = normed_local.shape[1] // chunks
+    sums = [None, None, None]
+    for c in range(chunks):
+        part = lax.all_gather(
+            normed_local[:, c * width : (c + 1) * width], "tp", axis=0, tiled=True
+        )
+        for i, w in enumerate((w_query, w_key, w_value)):
+            term = jnp.dot(part, w[c * width : (c + 1) * width], preferred_element_type=jnp.float32)
+            sums[i] = term if sums[i] is None else sums[i] + term
+    query = (sums[0] + qkv_bias[0]) * HEAD_DIM ** (-0.5)
+    keys = jnp.where(live[:, None], sums[1] + qkv_bias[1], 0.0)
+    values = jnp.where(live[:, None], sums[2] + qkv_bias[2], 0.0)
+    return (query.astype(jnp.bfloat16), keys.astype(jnp.bfloat16), values.astype(jnp.bfloat16))
+
+
 def on_device(
     hidden_in, ln_gain, ln_bias, w_query, w_key, w_value, qkv_bias, segment_ids, page_table
 ):
-    projected = project(
-        layer_norm(lax.all_gather(hidden_in, "tp", axis=0, tiled=True), ln_gain, ln_bias),
+    query, keys, values = project_chunks(
+        layer_norm(hidden_in, ln_gain, ln_bias),
         w_query,
         w_key,
         w_value,
         qkv_bias,
         segment_ids >= 0,
+        CHUNKS,
     )
-    query, keys, values = (projected[0], projected[1], projected[2])
     context = attend(query, keys, values, segment_ids)
     kv_cache = send_pages(keys, values, page_table)
     return (context, kv_cache)

time: 303 us -> 304 us (level)
  other arithmetic: 48 us -> 18 us
  waiting for transfers between devices: 139 us -> 164 us
  matrix products: 60.8 us -> 72 us
  local copies, waits for them, and re-layouts: 24.3 us -> 19.9 us
    all_gather x1 -> x4, waiting for transfers between devices: 133 us -> 155 us  [project_chunks(): lax.all_gather(normed_local[:, c * width:(c + 1) * width], 'tp', axis=0,...]
    convert_element_type x1, other arithmetic: 15.6 us -> 0.77 us  [layer_norm(): (center * lax.rsqrt(spread + 1e-05) * gain + shift).astype(jnp.bfloat16)]
    dot_general x3 -> x12, matrix products: 39.6 us -> 50.9 us  [project_chunks(): jnp.dot(part, w[c * width:(c + 1) * width], preferred_element_type=jnp.fl...]
    reduce_sum x1, other arithmetic: 9.1 us -> 2.14 us  [layer_norm(): spread = jnp.mean(center * center, axis=1, keepdims=True)]
    reduce_sum x1, other arithmetic: 7.49 us -> 1.94 us  [layer_norm(): center = values - jnp.mean(values, axis=1, keepdims=True)]
    another operation x4, local copies, waits for them, and re-layouts: 6.55 us -> 2.03 us  [send_pages(): jnp.stack([keys, values], axis=0)]
    reshape x2 -> x3, local copies, waits for them, and re-layouts: 6.18 us -> 3.98 us  [split(): return array.reshape(positions, heads, HEAD_DIM).transpose(1, 0, 2)]
  transfers between devices with their start and end apart: 3 -> 6, of which waited for: 2 -> 5; matrix products, arithmetic and copies ran while one was open for 13% -> 18% of each run, Pallas kernels for 0% -> 0%
where the time goes in v1:
time: 304 us
  waiting for transfers between devices  164 us (54%)
  matrix products  72 us (24%)
  local copies, waits for them, and re-layouts  19.9 us (7%)
  other arithmetic  18 us (6%)
  starting transfers between devices  15.9 us (5%)
  between operations  14.2 us (5%)
    all_gather x4, waiting for transfers between devices, project_chunks(): lax.all_gather(normed_local[:, c * width:(c + 1) * width], 'tp', axis=0,...  155 us
    dot_general x12, matrix products, project_chunks(): jnp.dot(part, w[c * width:(c + 1) * width], preferred_element_type=jnp.fl...  50.9 us
    dot_general x4, matrix products, head_rows(): scores = jnp.dot(query_head, key_head.T, preferred_element_type=jnp.float32)  11.8 us
    dot_general x4, matrix products, head_rows(): jnp.dot(probs, value_head, preferred_element_type=jnp.float32)  9.27 us
    all_to_all x1, starting transfers between devices, send_pages(): lax.all_to_all(local_slot[order], 'req', split_axis=0, concat_axis=0, til...  8.44 us
    reduce_sum x4, other arithmetic, head_rows(): total = jnp.maximum(jnp.sum(weights, axis=1, keepdims=True), 1.0)  8.14 us
    all_to_all x1, starting transfers between devices, send_pages(): lax.all_to_all(stacked[order], 'req', split_axis=0, concat_axis=0, tiled=...  7.27 us
    all_to_all x1, waiting for transfers between devices, send_pages(): lax.all_to_all(local_slot[order], 'req', split_axis=0, concat_axis=0, til...  7.14 us
  transfers between devices with their start and end apart: 6, of which 5 were waited for; matrix products, arithmetic and copies ran while one was open for 18% of the time, Pallas kernels for 0%

profile of v1, /device:TPU:1, one launch (start us, length us, event | category | flops | bytes accessed | tf_op | source)
XLA Modules:
  0.0 303.6 jit_solution(23580212619107759)
XLA Ops:
  19.1 8.4 %all-to-all-start.1 = ((s32[16,4,1]{1,2,0:T(1,128)}), s32[16,4,1]{1,2,0:T(1,128)S(1)}, u32[]{:S(2)}, u32[]{:S(2)}) async-start(s32[16,4,1]{1,2,0:T(1,128)} %bitcast.15), calls=%async_computation.1 | async-start | bytes 16384 | tf_op jit(solution)/shard_map/all_to_all | solution.py:65
  27.6 7.1 %all-to-all-done.1 = s32[16,4,1]{1,2,0:T(1,128)S(1)} async-done(((s32[16,4,1]{1,2,0:T(1,128)}), s32[16,4,1]{1,2,0:T(1,128)S(1)}, u32[]{:S(2)}, u32[]{:S(2)}) %all-to-all-start.1) | async-done | bytes 288 | tf_op jit(solution)/shard_map/all_to_all | solution.py:65
  38.0 26.6 %all-gather.11.cloned.1.call-done = bf16[1024,1792]{1,0:T(8,128)(2,1)} async-done(((bf16[128,1792]{1,0:T(8,128)(2,1)}), bf16[1024,1792]{1,0:T(8,128)(2,1)}) %all-gather.11.cloned.1.call-update) | async-done | bytes 3670032 | tf_op jit(solution)/shard_map/all_gather | solution.py:75
  64.6 6.0 %fusion.21 = f32[1024,512]{0,1:T(8,128)} fusion(bf16[1024,1792]{1,0:T(8,128)(2,1)} %all-gather.11.cloned.1.call-done, bf16[7168,512]{1,0:T(8,128)(2,1)} %param.16), kind=kOutput, calls=%fused_computation.36 | convolution fusion | flops 1879048192 | bytes 7602176 | tf_op jit(solution)/shard_map/dot_general | solution.py:79
  70.6 42.7 %all-gather.9.cloned.1.call-done = bf16[1024,1792]{1,0:T(8,128)(2,1)} async-done(((bf16[128,1792]{1,0:T(8,128)(2,1)}), bf16[1024,1792]{1,0:T(8,128)(2,1)}) %all-gather.9.cloned.1.call-update) | async-done | bytes 3670032 | tf_op jit(solution)/shard_map/all_gather | solution.py:75
  113.3 6.0 %fusion.23 = f32[1024,512]{0,1:T(8,128)} fusion(bf16[1024,1792]{1,0:T(8,128)(2,1)} %all-gather.9.cloned.1.call-done, bf16[7168,512]{1,0:T(8,128)(2,1)} %param.16), kind=kOutput, calls=%fused_computation.38 | convolution fusion | flops 1879048192 | bytes 7602176 | tf_op jit(solution)/shard_map/dot_general | solution.py:79
  119.3 42.7 %all-gather.7.cloned.1.call-done = bf16[1024,1792]{1,0:T(8,128)(2,1)} async-done(((bf16[128,1792]{1,0:T(8,128)(2,1)}), bf16[1024,1792]{1,0:T(8,128)(2,1)}) %all-gather.7.cloned.1.call-update) | async-done | bytes 3670032 | tf_op jit(solution)/shard_map/all_gather | solution.py:75
  162.0 6.0 %fusion.25 = f32[1024,512]{0,1:T(8,128)} fusion(bf16[1024,1792]{1,0:T(8,128)(2,1)} %all-gather.7.cloned.1.call-done, bf16[7168,512]{1,0:T(8,128)(2,1)} %param.16), kind=kOutput, calls=%fused_computation.40 | convolution fusion | flops 1879048192 | bytes 7602176 | tf_op jit(solution)/shard_map/dot_general | solution.py:79
  168.0 42.5 %all-gather.5.cloned.1.call-done = bf16[1024,1792]{1,0:T(8,128)(2,1)} async-done(((bf16[128,1792]{1,0:T(8,128)(2,1)}), bf16[1024,1792]{1,0:T(8,128)(2,1)}) %all-gather.5.cloned.1.call-update) | async-done | bytes 3670032 | tf_op jit(solution)/shard_map/all_gather | solution.py:75
  210.6 6.6 %select_convert_fusion = bf16[1024,512]{0,1:T(8,128)(2,1)S(1)} fusion(f32[1024,512]{0,1:T(8,128)} %fusion.21, f32[1024,512]{0,1:T(8,128)} %fusion.23, f32[1024,512]{0,1:T(8,128)} %fusion.25, bf16[1024,1792]{1,0:T(8,128)(2,1)} %all-gather.5.cloned.1.call-done, bf16[7168,512]{1,0:T(8,128)(2,1)} %param.16, f32[512]{0:T(512)S(1)} %bitcast.66, ...), kind=kOutput, calls=%fused_computation.33 | convolution fusion | flops 1882193920 | bytes 12848128 | tf_op jit(solution)/shard_map/dot_general | solution.py:79
  219.1 4.8 %fusion.29 = f32[1024,512]{0,1:T(8,128)S(1)} fusion(bf16[1024,1792]{1,0:T(8,128)(2,1)} %all-gather.11.cloned.1.call-done, bf16[7168,512]{1,0:T(8,128)(2,1)} %param.15), kind=kOutput, calls=%fused_computation.44 | convolution fusion | flops 1879048192 | bytes 7602176 | tf_op jit(solution)/shard_map/dot_general | solution.py:79
  224.0 3.8 %fusion.31 = f32[1024,512]{0,1:T(8,128)S(1)} fusion(bf16[1024,1792]{1,0:T(8,128)(2,1)S(1)} %copy-done.7, bf16[7168,512]{1,0:T(8,128)(2,1)} %param.15), kind=kOutput, calls=%fused_computation.46 | convolution fusion | flops 1879048192 | bytes 7602176 | tf_op jit(solution)/shard_map/dot_general | solution.py:79
  230.0 2.4 select_convert_fusion.1
  234.2 4.8 %fusion.37 = f32[1024,512]{0,1:T(8,128)S(1)} fusion(bf16[1024,1792]{1,0:T(8,128)(2,1)} %all-gather.11.cloned.1.call-done, bf16[7168,512]{1,0:T(8,128)(2,1)} %param.14), kind=kOutput, calls=%fused_computation.52 | convolution fusion | flops 1879048192 | bytes 7602176 | tf_op jit(solution)/shard_map/dot_general | solution.py:79
  239.1 3.8 %fusion.39 = f32[1024,512]{0,1:T(8,128)S(1)} fusion(bf16[1024,1792]{1,0:T(8,128)(2,1)S(1)} %copy-done.8, bf16[7168,512]{1,0:T(8,128)(2,1)} %param.14), kind=kOutput, calls=%fused_computation.54 | convolution fusion | flops 1879048192 | bytes 7602176 | tf_op jit(solution)/shard_map/dot_general | solution.py:79
  245.1 2.4 multiply_convert_fusion
  253.9 7.3 %all-to-all-start = ((bf16[64,2,16,4,128]{4,2,3,1,0:T(8,128)(2,1)}), bf16[64,2,16,4,128]{4,2,3,1,0:T(8,128)(2,1)S(1)}, u32[]{:S(2)}, u32[]{:S(2)}) async-start(bf16[64,2,16,4,128]{4,2,3,1,0:T(8,128)(2,1)} %gather_fusion), calls=%async_computation | async-start | bytes 4194304 | tf_op jit(solution)/shard_map/all_to_all | solution.py:64
  261.2 29.4 %while.10 = (s32[]{:T(128)}, bf16[4,1024,128]{2,1,0:T(8,128)(2,1)S(1)}, s32[1024]{0:T(1024)S(1)}, bf16[4,1024,128]{2,1,0:T(8,128)(2,1)}, bf16[4,1024,128]{2,1,0:...) while((s32[]{:T(128)}, bf16[4,1024,128]{2,1,0:T(8,128)(2,1)S(1)}, s32[1024]{0:T(1024)S(1)}, ...), condition=%wide.region_5.6_spmd, body=%wide.region_2.5_spmd.sunk | while | flops 559022080 | bytes 13690957 | solution.py:43
  261.2 2.9 fusion.72
  266.2 2.3 fusion.74
  268.5 2.9 fusion.72
  275.9 2.9 fusion.72
  283.2 2.9 fusion.72
  293.8 3.3 %copy.33 = bf16[2,4,64,16,128]{4,3,2,1,0:T(8,128)(2,1)} copy(bf16[2,4,64,16,128]{4,3,1,0,2:T(8,128)(2,1)} %bitcast.57) | data formatting | bytes 4194304
  (100 shorter events, 47.8 us)
Async XLA Ops:
  7.2 4.2 %copy-start = (bf16[128,7168]{1,0:T(8,128)(2,1)S(1)}, bf16[128,7168]{1,0:T(8,128)(2,1)}, u32[]{:S(2)}) copy-start(bf16[128,7168]{1,0:T(8,128)(2,1)} %param.11) | copy-start | bytes 5505028
  7.2 4.2 %copy-start.5 = (f32[7168]{0:T(1024)S(1)}, f32[7168]{0:T(1024)}, u32[]{:S(2)}) copy-start(f32[7168]{0:T(1024)} %param.12) | copy-start | bytes 86020
  7.2 4.2 %copy-start.4 = (f32[7168]{0:T(1024)S(1)}, f32[7168]{0:T(1024)}, u32[]{:S(2)}) copy-start(f32[7168]{0:T(1024)} %param.13) | copy-start | bytes 86020
  7.2 57.4 %all-gather.11.cloned.1.call-start = ((), (), s32[]{:S(2)}) async-start(), calls=%async_computation.5 | async-start | bytes 4128768 | tf_op jit(solution)/shard_map/all_gather | solution.py:75
  12.2 3.4 %copy-start.13 = (s32[64]{0:T(128)S(1)}, s32[64]{0:T(128)}, u32[]{:S(2)}) copy-start(s32[64]{0:T(128)} %param.19) | copy-start | bytes 772
  12.2 15.4 %copy-start.6 = (f32[3,512]{1,0:T(4,128)S(1)}, f32[3,512]{1,0:T(4,128)}, u32[]{:S(2)}) copy-start(f32[3,512]{1,0:T(4,128)} %param.17) | copy-start | bytes 18436
  12.2 15.4 %copy-start.2 = (s32[1024]{0:T(1024)S(1)}, s32[1024]{0:T(1024)}, u32[]{:S(2)}) copy-start(s32[1024]{0:T(1024)} %param.18) | copy-start | bytes 12292
  13.5 99.8 %all-gather.9.cloned.1.call-start = ((), (), s32[]{:S(2)}) async-start(), calls=%async_computation.4 | async-start | bytes 4128768 | tf_op jit(solution)/shard_map/all_gather | solution.py:75
  14.3 147.8 %all-gather.7.cloned.1.call-start = ((), (), s32[]{:S(2)}) async-start(), calls=%async_computation.3 | async-start | bytes 4128768 | tf_op jit(solution)/shard_map/all_gather | solution.py:75
  15.0 195.6 %all-gather.5.cloned.1.call-start = ((), (), s32[]{:S(2)}) async-start(), calls=%async_computation.2 | async-start | bytes 4128768 | tf_op jit(solution)/shard_map/all_gather | solution.py:75
  19.1 15.6 %all-to-all-start.1 = ((s32[16,4,1]{1,2,0:T(1,128)}), s32[16,4,1]{1,2,0:T(1,128)S(1)}, u32[]{:S(2)}, u32[]{:S(2)}) async-start(s32[16,4,1]{1,2,0:T(1,128)} %bitcast.15), calls=%async_computation.1 | async-start | bytes 16384 | tf_op jit(solution)/shard_map/all_to_all | solution.py:65
  219.1 4.9 %copy-start.7 = (bf16[1024,1792]{1,0:T(8,128)(2,1)S(1)}, bf16[1024,1792]{1,0:T(8,128)(2,1)}, u32[]{:S(2)}) copy-start(bf16[1024,1792]{1,0:T(8,128)(2,1)} %all-gather.9.cloned.1.call-done) | copy-start | bytes 11010052
  219.1 8.7 %slice-start = ((s8[7340032]{0:T(1024)(128)(4,1)}), s8[4194304]{0:T(1024)(128)(4,1)S(1)}, s32[]{:S(2)}) async-start(s8[7340032]{0:T(1024)(128)(4,1)} %bitcast.67), calls=%async_computation.6 | async-start | bytes 8388608
  224.0 3.8 %slice-start.1 = ((s8[7340032]{0:T(1024)(128)(4,1)}), s8[3145728]{0:T(1024)(128)(4,1)S(1)}, s32[]{:S(2)}) async-start(s8[7340032]{0:T(1024)(128)(4,1)} %bitcast.67), calls=%async_computation.7 | async-start | bytes 6291456
  224.0 3.8 %copy-start.9 = (bf16[1024,1792]{1,0:T(8,128)(2,1)S(1)}, bf16[1024,1792]{1,0:T(8,128)(2,1)}, u32[]{:S(2)}) copy-start(bf16[1024,1792]{1,0:T(8,128)(2,1)} %all-gather.7.cloned.1.call-done) | copy-start | bytes 11010052
  227.8 2.1 copy-start.11
  234.2 4.9 %copy-start.8 = (bf16[1024,1792]{1,0:T(8,128)(2,1)S(1)}, bf16[1024,1792]{1,0:T(8,128)(2,1)}, u32[]{:S(2)}) copy-start(bf16[1024,1792]{1,0:T(8,128)(2,1)} %all-gather.9.cloned.1.call-done) | copy-start | bytes 11010052
  234.2 8.7 %slice-start.2 = ((s8[7340032]{0:T(1024)(128)(4,1)}), s8[4194304]{0:T(1024)(128)(4,1)S(1)}, s32[]{:S(2)}) async-start(s8[7340032]{0:T(1024)(128)(4,1)} %bitcast.69), calls=%async_computation.8 | async-start | bytes 8388608
  239.1 3.8 %slice-start.3 = ((s8[7340032]{0:T(1024)(128)(4,1)}), s8[3145728]{0:T(1024)(128)(4,1)S(1)}, s32[]{:S(2)}) async-start(s8[7340032]{0:T(1024)(128)(4,1)} %bitcast.69), calls=%async_computation.9 | async-start | bytes 6291456
  239.1 3.8 %copy-start.10 = (bf16[1024,1792]{1,0:T(8,128)(2,1)S(1)}, bf16[1024,1792]{1,0:T(8,128)(2,1)}, u32[]{:S(2)}) copy-start(bf16[1024,1792]{1,0:T(8,128)(2,1)} %all-gather.7.cloned.1.call-done) | copy-start | bytes 11010052
  242.9 2.1 copy-start.12
  250.3 1.2 copy-start.1
  251.7 9.4 %copy-start.3 = (bf16[4,1024,128]{2,1,0:T(8,128)(2,1)S(1)}, bf16[4,1024,128]{2,1,0:T(8,128)(2,1)}, u32[]{:S(2)}) copy-start(bf16[4,1024,128]{2,1,0:T(8,128)(2,1)} %custom-call.6) | copy-start | bytes 3145732
  253.9 37.8 %all-to-all-start = ((bf16[64,2,16,4,128]{4,2,3,1,0:T(8,128)(2,1)}), bf16[64,2,16,4,128]{4,2,3,1,0:T(8,128)(2,1)S(1)}, u32[]{:S(2)}, u32[]{:S(2)}) async-start(bf16[64,2,16,4,128]{4,2,3,1,0:T(8,128)(2,1)} %gather_fusion), calls=%async_computation | async-start | bytes 4194304 | tf_op jit(solution)/shard_map/all_to_all | solution.py:64
Sparse Core Ops, SparseCore 0:
  13.6 50.9 all-gather.10
  66.2 47.0 all-gather.8
  114.9 47.0 all-gather.6
  163.5 47.0 all-gather.4

commit v2 on v1

--- a/solution.py
+++ b/solution.py
@@ -1,10 +1,14 @@
+import functools
+
 import jax
 import jax.numpy as jnp
 from jax import lax
+from jax.experimental import pallas as pl
 from jax.sharding import PartitionSpec as P
 
 HEAD_DIM = 128
-CHUNKS = 4
+CHUNKS = 2
+Q_BLOCK = 256
 
 
 def layer_norm(rows, gain, shift):
@@ -14,37 +18,51 @@
     return (center * lax.rsqrt(spread + 1e-05) * gain + shift).astype(jnp.bfloat16)
 
 
-def head_rows(query_head, key_head, value_head, segments, first, last):
-    count = key_head.shape[0]
-    query_pos = jnp.arange(first, last)
-    key_pos = jnp.arange(0, count)
-    visible = (
-        (segments[:, None] == segments[None, :])
-        & (segments[None, :] >= 0)
-        & (key_pos[None, :] <= query_pos[:, None])
-    )
-    scores = jnp.dot(query_head, key_head.T, preferred_element_type=jnp.float32)
-    scores = jnp.where(visible, scores, -1e30)
-    top = jnp.max(scores, axis=1, keepdims=True)
-    weights = jnp.where(visible, jnp.exp(scores - top), 0.0)
-    total = jnp.maximum(jnp.sum(weights, axis=1, keepdims=True), 1.0)
-    probs = (weights / total).astype(jnp.bfloat16)
-    return jnp.dot(probs, value_head, preferred_element_type=jnp.float32).astype(jnp.bfloat16)
+def attention_kernel(q_ref, k_ref, v_ref, segq_ref, segk_ref, o_ref, *, block):
+    qb = pl.program_id(1)
+    for b in range(k_ref.shape[0] // block):
+
+        @pl.when(qb == b)
+        def _():
+            n = (b + 1) * block
+            q = q_ref[...]
+            k = k_ref[0:n, :]
+            scores = lax.dot_general(
+                q, k, (((1,), (1,)), ((), ())), preferred_element_type=jnp.float32
+            )
+            seg_q = segq_ref[...]
+            seg_k = segk_ref[:, 0:n]
+            row = b * block + lax.broadcasted_iota(jnp.int32, (block, n), 0)
+            col = lax.broadcasted_iota(jnp.int32, (block, n), 1)
+            visible = (seg_q == seg_k) & (seg_k >= 0) & (col <= row)
+            scores = jnp.where(visible, scores, -1e30)
+            top = jnp.max(scores, axis=1, keepdims=True)
+            weights = jnp.where(visible, jnp.exp(scores - top), 0.0)
+            total = jnp.maximum(jnp.sum(weights, axis=1, keepdims=True), 1.0)
+            probs = (weights / total).astype(jnp.bfloat16)
+            o_ref[...] = jnp.dot(
+                probs, v_ref[0:n, :], preferred_element_type=jnp.float32
+            ).astype(o_ref.dtype)
 
 
 def attend(query, keys, values, segments):
     positions, width = query.shape
     heads = width // HEAD_DIM
-
-    def split(array):
-        return array.reshape(positions, heads, HEAD_DIM).transpose(1, 0, 2)
-
-    query_heads, key_heads, value_heads = (split(query), split(keys), split(values))
-    attended = lax.map(
-        lambda items: head_rows(items[0], items[1], items[2], segments, 0, positions),
-        (query_heads, key_heads, value_heads),
-    )
-    return attended.transpose(1, 0, 2).reshape(positions, width)
+    block = Q_BLOCK
+    kernel = functools.partial(attention_kernel, block=block)
+    return pl.pallas_call(
+        kernel,
+        grid=(heads, positions // block),
+        in_specs=[
+            pl.BlockSpec((block, HEAD_DIM), lambda h, i: (i, h)),
+            pl.BlockSpec((positions, HEAD_DIM), lambda h, i: (0, h)),
+            pl.BlockSpec((positions, HEAD_DIM), lambda h, i: (0, h)),
+            pl.BlockSpec((block, 1), lambda h, i: (i, 0)),
+            pl.BlockSpec((1, positions), lambda h, i: (0, 0)),
+        ],
+        out_specs=pl.BlockSpec((block, HEAD_DIM), lambda h, i: (i, h)),
+        out_shape=jax.ShapeDtypeStruct((positions, width), query.dtype),
+    )(query, keys, values, segments.reshape(positions, 1), segments.reshape(1, positions))
 
 
 def send_pages(keys, values, page_table):

time: 304 us -> 261 us (0.86)
  matrix products: 72 us -> 43.7 us
  waiting for transfers between devices: 164 us -> 145 us
  Pallas kernels: 0 us -> 16 us
  other arithmetic: 18 us -> 11.2 us
  local copies, waits for them, and re-layouts: 19.9 us -> 14.2 us
    dot_general x8 -> x0, matrix products: 21 us -> none  [the longest x4 11.8 us: head_rows(): scores = jnp.dot(query_head, key_head.T, preferred_element_type=jnp.float32)]
    all_gather x4 -> x2, waiting for transfers between devices: 155 us -> 138 us  [project_chunks(): lax.all_gather(normed_local[:, c * width:(c + 1) * width], 'tp', axis=0,...]
    pallas_call x0 -> x1, Pallas kernels: none -> 16 us  [attend(): pl.pallas_call(kernel, grid=(heads, positions // block), in_specs=[pl.Blo...]
    reduce_sum x4 -> x0, other arithmetic: 8.14 us -> none  [head_rows(): total = jnp.maximum(jnp.sum(weights, axis=1, keepdims=True), 1.0)]
    dot_general x12 -> x6, matrix products: 50.9 us -> 43.7 us  [project_chunks(): jnp.dot(part, w[c * width:(c + 1) * width], preferred_element_type=jnp.fl...]
    reshape x4 -> x1, local copies, waits for them, and re-layouts: 5.07 us -> 1.03 us  [attend(): segments.reshape(positions, 1)]
  transfers between devices with their start and end apart: 6 -> 4, of which waited for: 5 -> 3; matrix products, arithmetic and copies ran while one was open for 18% -> 12% of each run, Pallas kernels for 0% -> 6%
where the time goes in v2:
time: 261 us; the launch traced here: 260 us
  waiting for transfers between devices  145 us (56%)
  matrix products  43.7 us (17%)
  Pallas kernels  16 us (6%)
  starting transfers between devices  15.8 us (6%)
  between operations  14.4 us (6%)
  local copies, waits for them, and re-layouts  14.2 us (5%)
  other arithmetic  11.2 us (4%)
    all_gather x2, waiting for transfers between devices, project_chunks(): lax.all_gather(normed_local[:, c * width:(c + 1) * width], 'tp', axis=0,...  138 us
    dot_general x6, matrix products, project_chunks(): jnp.dot(part, w[c * width:(c + 1) * width], preferred_element_type=jnp.fl...  43.7 us
    pallas_call x1, Pallas kernels, attend(): pl.pallas_call(kernel, grid=(heads, positions // block), in_specs=[pl.Blo...  16 us
    all_to_all x1, starting transfers between devices, send_pages(): lax.all_to_all(local_slot[order], 'req', split_axis=0, concat_axis=0, til...  8.44 us
    all_to_all x1, starting transfers between devices, send_pages(): lax.all_to_all(stacked[order], 'req', split_axis=0, concat_axis=0, tiled=...  7.26 us
    all_to_all x1, waiting for transfers between devices, send_pages(): lax.all_to_all(local_slot[order], 'req', split_axis=0, concat_axis=0, til...  5.96 us
  transfers between devices with their start and end apart: 4, of which 3 were waited for; matrix products, arithmetic and copies ran while one was open for 12% of the time, Pallas kernels for 6%

profile of v2, /device:TPU:1, one launch (start us, length us, event | category | flops | bytes accessed | tf_op | source)
XLA Modules:
  0.0 260.0 jit_solution(3764472412127421237)
XLA Ops:
  7.2 1.9 convert_reduce_fusion
  9.2 2.1 fusion.2
  12.2 1.3 fusion.24
  14.3 2.1 sort.34
  16.5 0.8 gather_fusion.1
  17.9 8.4 %all-to-all-start.1 = ((s32[16,4,1]{1,2,0:T(1,128)}), s32[16,4,1]{1,2,0:T(1,128)S(1)}, u32[]{:S(2)}, u32[]{:S(2)}) async-start(s32[16,4,1]{1,2,0:T(1,128)} %bitcast.6), calls=%async_computation.1 | async-start | bytes 16384 | tf_op jit(solution)/shard_map/all_to_all | solution.py:83
  26.4 1.0 copy.17.segq_ref
  27.4 6.0 %all-to-all-done.1 = s32[16,4,1]{1,2,0:T(1,128)S(1)} async-done(((s32[16,4,1]{1,2,0:T(1,128)}), s32[16,4,1]{1,2,0:T(1,128)S(1)}, u32[]{:S(2)}, u32[]{:S(2)}) %all-to-all-start.1) | async-done | bytes 288 | tf_op jit(solution)/shard_map/all_to_all | solution.py:83
  34.7 2.1 sort.35
  36.8 62.3 %all-gather.5.cloned.1.call-done = bf16[1024,3584]{1,0:T(8,128)(2,1)} async-done(((bf16[128,3584]{1,0:T(8,128)(2,1)}), bf16[1024,3584]{1,0:T(8,128)(2,1)}) %all-gather.5.cloned.1.call-update) | async-done | bytes 7340048 | tf_op jit(solution)/shard_map/all_gather | solution.py:93
  99.1 7.3 %fusion.6 = f32[1024,512]{1,0:T(8,128)S(1)} fusion(bf16[1024,3584]{1,0:T(8,128)(2,1)} %all-gather.5.cloned.1.call-done, bf16[7168,512]{1,0:T(8,128)(2,1)} %param.14), kind=kOutput, calls=%fused_computation.11 | convolution fusion | flops 3758096384 | bytes 13107200 | tf_op jit(solution)/shard_map/dot_general | solution.py:97
  106.4 75.7 %all-gather.3.cloned.1.call-done = bf16[1024,3584]{1,0:T(8,128)(2,1)} async-done(((bf16[128,3584]{1,0:T(8,128)(2,1)}), bf16[1024,3584]{1,0:T(8,128)(2,1)}) %all-gather.3.cloned.1.call-update) | async-done | bytes 7340048 | tf_op jit(solution)/shard_map/all_gather | solution.py:93
  182.1 8.1 %select_convert_fusion.v_ref = bf16[1024,512]{1,0:T(8,128)(2,1)S(1)} fusion(f32[1024,512]{1,0:T(8,128)S(1)} %fusion.6, bf16[1024,3584]{1,0:T(8,128)(2,1)} %all-gather.3.cloned.1.call-done, bf16[7168,512]{1,0:T(8,128)(2,1)} %param.14, f32[512]{0:T(512)S(1)} %bitcast.21, pred[1024]{0:T(1024)(128)(4,1)S(1)} %broadcast_compare_fusion), kind=kOutput, calls=%fused_computation.24 | convolution fusion | flops 3760193536 | bytes 14158848 | tf_op jit(solution)/shard_map/dot_general | solution.py:97
  190.5 1.2 copy.19
  191.7 8.1 %fusion.10 = f32[1024,512]{1,0:T(8,128)S(1)} fusion(bf16[1024,3584]{1,0:T(8,128)(2,1)} %all-gather.5.cloned.1.call-done, bf16[7168,512]{1,0:T(8,128)(2,1)} %param.13), kind=kOutput, calls=%fused_computation.15 | convolution fusion | flops 3758096384 | bytes 13107200 | tf_op jit(solution)/shard_map/dot_general | solution.py:97
  199.9 3.9 %select_convert_fusion.1.k_ref = bf16[1024,512]{1,0:T(8,128)(2,1)S(1)} fusion(f32[1024,512]{1,0:T(8,128)S(1)} %fusion.10, bf16[1024,3584]{1,0:T(8,128)(2,1)S(1)} %bitcast.25, bf16[7168,512]{1,0:T(8,128)(2,1)S(1)} %bitcast.23, f32[512]{0:T(512)S(1)} %bitcast.20, pred[1024]{0:T(1024)(128)(4,1)S(1)} %broadcast_compare_fusion), kind=kOutput, calls=%fused_computation.25 | convolution fusion | flops 3760193536 | bytes 14158848 | tf_op jit(solution)/shard_map/dot_general | solution.py:97
  204.4 1.5 maximum_bitcast_fusion
  205.9 2.1 gather_fusion
  208.0 7.3 %all-to-all-start = ((bf16[64,2,16,4,128]{4,2,3,1,0:T(8,128)(2,1)}), bf16[64,2,16,4,128]{4,2,3,1,0:T(8,128)(2,1)S(1)}, u32[]{:S(2)}, u32[]{:S(2)}) async-start(bf16[64,2,16,4,128]{4,2,3,1,0:T(8,128)(2,1)} %gather_fusion), calls=%async_computation | async-start | bytes 4194304 | tf_op jit(solution)/shard_map/all_to_all | solution.py:82
  215.3 7.3 %fusion.14 = f32[1024,512]{1,0:T(8,128)S(1)} fusion(bf16[1024,3584]{1,0:T(8,128)(2,1)} %all-gather.5.cloned.1.call-done, bf16[7168,512]{1,0:T(8,128)(2,1)} %param.12), kind=kOutput, calls=%fused_computation.19 | convolution fusion | flops 3758096384 | bytes 13107200 | tf_op jit(solution)/shard_map/dot_general | solution.py:97
  222.6 9.1 %multiply_convert_fusion.q_ref = bf16[1024,512]{1,0:T(8,128)(2,1)} fusion(f32[1024,512]{1,0:T(8,128)S(1)} %fusion.14, bf16[1024,3584]{1,0:T(8,128)(2,1)} %all-gather.3.cloned.1.call-done, bf16[7168,512]{1,0:T(8,128)(2,1)} %param.12, f32[512]{0:T(512)S(1)} %bitcast.19), kind=kOutput, calls=%fused_computation.26 | convolution fusion | flops 3760193536 | bytes 14157824 | tf_op jit(solution)/shard_map/dot_general | solution.py:97
  231.6 16.0 %shard_map.104 = bf16[1024,512]{1,0:T(8,128)(2,1)} custom-call(bf16[1024,512]{1,0:T(8,128)(2,1)} %multiply_convert_fusion.q_ref, bf16[1024,512]{1,0:T(8,128)(2,1)} %copy-done.2, bf16[1024,512]{1,0:T(8,128)(2,1)} %copy-done.1, s32[1024,1]{1,0:T(8,128)} %copy.17.segq_ref, s32[1,1024]{1,0:T(1,128)} %bitcast.17), custom_call_target="tpu_custom_call" | custom-call | tf_op jit(solution)/shard_map/pallas_call | solution.py:53
  247.7 2.1 gather_fusion.2
  249.8 3.3 %copy.21 = bf16[2,4,64,16,128]{4,3,2,1,0:T(8,128)(2,1)} copy(bf16[2,4,64,16,128]{4,3,1,0,2:T(8,128)(2,1)} %bitcast.16) | data formatting | bytes 4194304
  (50 shorter events, 4.5 us)
Async XLA Ops:
  7.2 4.2 %copy-start = (bf16[128,7168]{1,0:T(8,128)(2,1)S(1)}, bf16[128,7168]{1,0:T(8,128)(2,1)}, u32[]{:S(2)}) copy-start(bf16[128,7168]{1,0:T(8,128)(2,1)} %param.9) | copy-start | bytes 5505028
  7.2 4.2 %copy-start.5 = (f32[7168]{0:T(1024)S(1)}, f32[7168]{0:T(1024)}, u32[]{:S(2)}) copy-start(f32[7168]{0:T(1024)} %param.10) | copy-start | bytes 86020
  7.2 4.2 %copy-start.4 = (f32[7168]{0:T(1024)S(1)}, f32[7168]{0:T(1024)}, u32[]{:S(2)}) copy-start(f32[7168]{0:T(1024)} %param.11) | copy-start | bytes 86020
  7.2 91.9 %all-gather.5.cloned.1.call-start = ((), (), s32[]{:S(2)}) async-start(), calls=%async_computation.3 | async-start | bytes 8257536 | tf_op jit(solution)/shard_map/all_gather | solution.py:93
  12.1 2.2 copy-start.7
  12.2 14.2 %copy-start.6 = (f32[3,512]{1,0:T(4,128)S(1)}, f32[3,512]{1,0:T(4,128)}, u32[]{:S(2)}) copy-start(f32[3,512]{1,0:T(4,128)} %param.15) | copy-start | bytes 18436
  12.2 14.2 %copy-start.3 = (s32[1024]{0:T(1024)S(1)}, s32[1024]{0:T(1024)}, u32[]{:S(2)}) copy-start(s32[1024]{0:T(1024)} %param.16) | copy-start | bytes 12292
  13.5 168.6 %all-gather.3.cloned.1.call-start = ((), (), s32[]{:S(2)}) async-start(), calls=%async_computation.2 | async-start | bytes 8257536 | tf_op jit(solution)/shard_map/all_gather | solution.py:93
  17.9 15.5 %all-to-all-start.1 = ((s32[16,4,1]{1,2,0:T(1,128)}), s32[16,4,1]{1,2,0:T(1,128)S(1)}, u32[]{:S(2)}, u32[]{:S(2)}) async-start(s32[16,4,1]{1,2,0:T(1,128)} %bitcast.6), calls=%async_computation.1 | async-start | bytes 16384 | tf_op jit(solution)/shard_map/all_to_all | solution.py:83
  190.2 9.6 %copy-start.1 = (bf16[1024,512]{1,0:T(8,128)(2,1)}, bf16[1024,512]{1,0:T(8,128)(2,1)S(1)}, u32[]{:S(2)}) copy-start(bf16[1024,512]{1,0:T(8,128)(2,1)S(1)} %select_convert_fusion.v_ref) | copy-start | bytes 3145732
  190.5 9.3 %slice-start = ((s8[7340032]{0:T(1024)(128)(4,1)}), s8[4194304]{0:T(1024)(128)(4,1)S(1)}, s32[]{:S(2)}) async-start(s8[7340032]{0:T(1024)(128)(4,1)} %bitcast.22), calls=%async_computation.4 | async-start | bytes 8388608
  190.5 9.3 %slice-start.2 = ((s8[7340032]{0:T(1024)(128)(4,1)}), s8[4194304]{0:T(1024)(128)(4,1)S(1)}, s32[]{:S(2)}) async-start(s8[7340032]{0:T(1024)(128)(4,1)} %bitcast.24), calls=%async_computation.6 | async-start | bytes 8388608
  191.7 8.1 %slice-start.1 = ((s8[7340032]{0:T(1024)(128)(4,1)}), s8[3145728]{0:T(1024)(128)(4,1)S(1)}, s32[]{:S(2)}) async-start(s8[7340032]{0:T(1024)(128)(4,1)} %bitcast.22), calls=%async_computation.5 | async-start | bytes 6291456
  191.7 8.1 %slice-start.3 = ((s8[7340032]{0:T(1024)(128)(4,1)}), s8[3145728]{0:T(1024)(128)(4,1)S(1)}, s32[]{:S(2)}) async-start(s8[7340032]{0:T(1024)(128)(4,1)} %bitcast.24), calls=%async_computation.7 | async-start | bytes 6291456
  203.8 2.1 copy-start.2
  208.0 39.7 %all-to-all-start = ((bf16[64,2,16,4,128]{4,2,3,1,0:T(8,128)(2,1)}), bf16[64,2,16,4,128]{4,2,3,1,0:T(8,128)(2,1)S(1)}, u32[]{:S(2)}, u32[]{:S(2)}) async-start(bf16[64,2,16,4,128]{4,2,3,1,0:T(8,128)(2,1)} %gather_fusion), calls=%async_computation | async-start | bytes 4194304 | tf_op jit(solution)/shard_map/all_to_all | solution.py:82
Sparse Core Ops, SparseCore 0:
  13.7 85.3 all-gather.4
  101.3 80.7 all-gather.2

commit v3 on v2

--- a/solution.py
+++ b/solution.py
@@ -7,7 +7,7 @@
 from jax.sharding import PartitionSpec as P
 
 HEAD_DIM = 128
-CHUNKS = 2
+SPLIT = 6144
 Q_BLOCK = 256
 
 
@@ -39,7 +39,7 @@
             top = jnp.max(scores, axis=1, keepdims=True)
             weights = jnp.where(visible, jnp.exp(scores - top), 0.0)
             total = jnp.maximum(jnp.sum(weights, axis=1, keepdims=True), 1.0)
-            probs = (weights / total).astype(jnp.bfloat16)
+            probs = (weights * (1.0 / total)).astype(jnp.bfloat16)
             o_ref[...] = jnp.dot(
                 probs, v_ref[0:n, :], preferred_element_type=jnp.float32
             ).astype(o_ref.dtype)
@@ -86,16 +86,15 @@
     return placed.transpose(1, 3, 0, 2, 4)
 
 
-def project_chunks(normed_local, w_query, w_key, w_value, qkv_bias, live, chunks):
-    width = normed_local.shape[1] // chunks
+def project_chunks(normed_local, w_query, w_key, w_value, qkv_bias, live, bounds):
     sums = [None, None, None]
-    for c in range(chunks):
-        part = lax.all_gather(
-            normed_local[:, c * width : (c + 1) * width], "tp", axis=0, tiled=True
-        )
+    for lo, hi in zip(bounds[:-1], bounds[1:]):
+        part = lax.all_gather(normed_local[:, lo:hi], "tp", axis=0, tiled=True)
         for i, w in enumerate((w_query, w_key, w_value)):
-            term = jnp.dot(part, w[c * width : (c + 1) * width], preferred_element_type=jnp.float32)
+            term = jnp.dot(part, w[lo:hi], preferred_element_type=jnp.float32)
             sums[i] = term if sums[i] is None else sums[i] + term
+        if hi < bounds[-1]:
+            sums = list(lax.optimization_barrier(tuple(sums)))
     query = (sums[0] + qkv_bias[0]) * HEAD_DIM ** (-0.5)
     keys = jnp.where(live[:, None], sums[1] + qkv_bias[1], 0.0)
     values = jnp.where(live[:, None], sums[2] + qkv_bias[2], 0.0)
@@ -112,7 +111,7 @@
         w_value,
         qkv_bias,
         segment_ids >= 0,
-        CHUNKS,
+        (0, SPLIT, hidden_in.shape[1]),
     )
     context = attend(query, keys, values, segment_ids)
     kv_cache = send_pages(keys, values, page_table)

time: 261 us -> 251 us (0.962)
  waiting for transfers between devices: 145 us -> 131 us
  starting transfers between devices: 15.8 us -> 21.3 us
  local copies, waits for them, and re-layouts: 14.2 us -> 18.8 us
  matrix products: 43.7 us -> 40.6 us
  other arithmetic: 11.2 us -> 8.34 us
    all_gather x2, waiting for transfers between devices: 138 us -> 128 us  [project_chunks(): part = lax.all_gather(normed_local[:, lo:hi], 'tp', axis=0, tiled=True)]
    all_to_all x1, waiting for transfers between devices: 5.96 us -> 0.01 us  [send_pages(): lax.all_to_all(local_slot[order], 'req', split_axis=0, concat_axis=0, til...]
    all_to_all x1, starting transfers between devices: 7.26 us -> 12.7 us  [send_pages(): lax.all_to_all(stacked[order], 'req', split_axis=0, concat_axis=0, tiled=...]
    all_to_all x1, waiting for transfers between devices: 0.01 us -> 3.14 us  [send_pages(): lax.all_to_all(stacked[order], 'req', split_axis=0, concat_axis=0, tiled=...]
    dot_general x6, matrix products: 43.7 us -> 40.6 us  [project_chunks(): term = jnp.dot(part, w[lo:hi], preferred_element_type=jnp.float32)]
    unnamed x25 -> x29, local copies, waits for them, and re-layouts: 3.35 us -> 6.39 us
  transfers between devices with their start and end apart: 4 -> 4, of which waited for: 3 -> 3; matrix products, arithmetic and copies ran while one was open for 12% -> 21% of each run, Pallas kernels for 6% -> 6%
where the time goes in v3:
time: 251 us
  waiting for transfers between devices  131 us (52%)
  matrix products  40.6 us (16%)
  starting transfers between devices  21.3 us (8%)
  local copies, waits for them, and re-layouts  18.8 us (7%)
  Pallas kernels  16 us (6%)
  between operations  14.3 us (6%)
  other arithmetic  8.34 us (3%)
    all_gather x2, waiting for transfers between devices, project_chunks(): part = lax.all_gather(normed_local[:, lo:hi], 'tp', axis=0, tiled=True)  128 us
    dot_general x6, matrix products, project_chunks(): term = jnp.dot(part, w[lo:hi], preferred_element_type=jnp.float32)  40.6 us
    pallas_call x1, Pallas kernels, attend(): pl.pallas_call(kernel, grid=(heads, positions // block), in_specs=[pl.Blo...  16 us
    all_to_all x1, starting transfers between devices, send_pages(): lax.all_to_all(stacked[order], 'req', split_axis=0, concat_axis=0, tiled=...  12.7 us
    all_to_all x1, starting transfers between devices, send_pages(): lax.all_to_all(local_slot[order], 'req', split_axis=0, concat_axis=0, til...  8.44 us
    unnamed x29, local copies, waits for them, and re-layouts  6.39 us
  transfers between devices with their start and end apart: 4, of which 3 were waited for; matrix products, arithmetic and copies ran while one was open for 21% of the time, Pallas kernels for 6%

profile of v3, /device:TPU:1, one launch (start us, length us, event | category | flops | bytes accessed | tf_op | source)
XLA Modules:
  0.0 250.8 jit_solution(8193423470042560862)
XLA Ops:
  7.2 1.9 convert_reduce_fusion
  10.7 1.2 copy-done.1
  11.9 1.3 slice.50
  13.2 2.0 sort.34
  16.7 8.4 %all-to-all-start.1 = ((s32[16,4,1]{1,2,0:T(1,128)}), s32[16,4,1]{1,2,0:T(1,128)S(1)}, u32[]{:S(2)}, u32[]{:S(2)}) async-start(s32[16,4,1]{1,2,0:T(1,128)} %bitcast.6), calls=%async_computation.1 | async-start | bytes 16384 | tf_op jit(solution)/shard_map/all_to_all | solution.py:83
  25.4 1.7 slice.51
  27.2 120.7 %all-gather.3.cloned.1.call-done = bf16[1024,6144]{1,0:T(8,128)(2,1)} async-done(((bf16[128,6144]{1,0:T(8,128)(2,1)}), bf16[1024,6144]{1,0:T(8,128)(2,1)}) %all-gather.3.cloned.1.call-update) | async-done | bytes 12582928 | tf_op jit(solution)/shard_map/all_gather | solution.py:92
  147.9 11.6 %fusion = f32[1024,512]{1,0:T(8,128)S(1)} fusion(bf16[1024,6144]{1,0:T(8,128)(2,1)} %all-gather.3.cloned.1.call-done, bf16[7168,512]{1,0:T(8,128)(2,1)} %param.14), kind=kOutput, calls=%fused_computation.3 | convolution fusion | flops 6442450944 | bytes 20971520 | tf_op jit(solution)/shard_map/dot_general | solution.py:94
  159.5 10.0 %fusion.2 = f32[1024,512]{1,0:T(8,128)} fusion(bf16[1024,6144]{1,0:T(8,128)(2,1)S(1)} %copy-done.9, bf16[7168,512]{1,0:T(8,128)(2,1)} %param.13), kind=kOutput, calls=%fused_computation.5 | convolution fusion | flops 6442450944 | bytes 20971520 | tf_op jit(solution)/shard_map/dot_general | solution.py:94
  169.5 8.0 %fusion.4 = f32[1024,512]{1,0:T(8,128)} fusion(bf16[1024,6144]{1,0:T(8,128)(2,1)S(1)} %copy-done.9, bf16[7168,512]{1,0:T(8,128)(2,1)S(1)} %bitcast.23), kind=kOutput, calls=%fused_computation.7 | convolution fusion | flops 6442450944 | bytes 20971520 | tf_op jit(solution)/shard_map/dot_general | solution.py:94
  177.4 7.4 %all-gather.5.cloned.1.call-done = bf16[1024,1024]{1,0:T(8,128)(2,1)} async-done(((bf16[128,1024]{1,0:T(8,128)(2,1)}), bf16[1024,1024]{1,0:T(8,128)(2,1)}) %all-gather.5.cloned.1.call-update) | async-done | bytes 2097168 | tf_op jit(solution)/shard_map/all_gather | solution.py:92
  184.9 3.1 %select_convert_fusion.v_ref = bf16[1024,512]{1,0:T(8,128)(2,1)S(1)} fusion(f32[1024,512]{1,0:T(8,128)S(1)} %fusion, bf16[1024,1024]{1,0:T(8,128)(2,1)} %all-gather.5.cloned.1.call-done, f32[512]{0:T(512)S(1)} %bitcast.21, bf16[7168,512]{1,0:T(8,128)(2,1)} %param.14, pred[1024]{0:T(1024)(128)(4,1)S(1)} %broadcast_compare_fusion), kind=kOutput, calls=%fused_computation.18 | convolution fusion | flops 1075838976 | bytes 6294528 | tf_op jit(solution)/shard_map/dot_general | solution.py:94
  188.3 1.2 copy.19
  189.6 0.8 copy-done.10
  190.3 3.2 %select_convert_fusion.1.k_ref = bf16[1024,512]{1,0:T(8,128)(2,1)S(1)} fusion(f32[1024,512]{1,0:T(8,128)} %fusion.2, bf16[1024,1024]{1,0:T(8,128)(2,1)S(1)} %copy-done.10, f32[512]{0:T(512)S(1)} %bitcast.20, bf16[7168,512]{1,0:T(8,128)(2,1)} %param.13, pred[1024]{0:T(1024)(128)(4,1)S(1)} %broadcast_compare_fusion), kind=kOutput, calls=%fused_computation.19 | convolution fusion | flops 1075838976 | bytes 6294528 | tf_op jit(solution)/shard_map/dot_general | solution.py:94
  195.3 2.1 gather_fusion
  197.5 12.7 %all-to-all-start = ((bf16[64,2,16,4,128]{4,2,3,1,0:T(8,128)(2,1)}), bf16[64,2,16,4,128]{4,2,3,1,0:T(8,128)(2,1)S(1)}, u32[]{:S(2)}, u32[]{:S(2)}) async-start(bf16[64,2,16,4,128]{4,2,3,1,0:T(8,128)(2,1)} %gather_fusion), calls=%async_computation | async-start | bytes 4194304 | tf_op jit(solution)/shard_map/all_to_all | solution.py:82
  210.1 1.1 copy.17.segq_ref
  212.5 2.0 sort.35
  214.5 4.8 %multiply_convert_fusion.q_ref = bf16[1024,512]{1,0:T(8,128)(2,1)} fusion(f32[1024,512]{1,0:T(8,128)} %fusion.4, bf16[1024,1024]{1,0:T(8,128)(2,1)} %all-gather.5.cloned.1.call-done, f32[512]{0:T(512)S(1)} %bitcast.19, bf16[7168,512]{1,0:T(8,128)(2,1)} %param.12), kind=kOutput, calls=%fused_computation.20 | convolution fusion | flops 1075838976 | bytes 6293504 | tf_op jit(solution)/shard_map/dot_general | solution.py:94
  219.3 16.0 %shard_map.104 = bf16[1024,512]{1,0:T(8,128)(2,1)} custom-call(bf16[1024,512]{1,0:T(8,128)(2,1)} %multiply_convert_fusion.q_ref, bf16[1024,512]{1,0:T(8,128)(2,1)} %copy-done.3, bf16[1024,512]{1,0:T(8,128)(2,1)} %copy-done.2, s32[1024,1]{1,0:T(8,128)} %copy.17.segq_ref, s32[1,1024]{1,0:T(1,128)} %bitcast.17), custom_call_target="tpu_custom_call" | custom-call | tf_op jit(solution)/shard_map/pallas_call | solution.py:53
  235.3 3.1 %all-to-all-done = bf16[64,2,16,4,128]{4,2,3,1,0:T(8,128)(2,1)S(1)} async-done(((bf16[64,2,16,4,128]{4,2,3,1,0:T(8,128)(2,1)}), bf16[64,2,16,4,128]{4,2,3,1,0:T(8,128)(2,1)S(1)}, u32[]{:S(2)}, u32[]{:S(2)}) %all-to-all-start) | async-done | bytes 2097184 | tf_op jit(solution)/shard_map/all_to_all | solution.py:82
  238.5 2.1 gather_fusion.2
  240.6 3.3 %copy.21 = bf16[2,4,64,16,128]{4,3,2,1,0:T(8,128)(2,1)} copy(bf16[2,4,64,16,128]{4,3,1,0,2:T(8,128)(2,1)} %bitcast.16) | data formatting | bytes 4194304
  (54 shorter events, 6.6 us)
Async XLA Ops:
  7.2 2.1 copy-start
  7.2 2.7 %copy-start.7 = (f32[7168]{0:T(1024)S(1)}, f32[7168]{0:T(1024)}, u32[]{:S(2)}) copy-start(f32[7168]{0:T(1024)} %param.10) | copy-start | bytes 86020
  7.2 2.7 %copy-start.6 = (f32[7168]{0:T(1024)S(1)}, f32[7168]{0:T(1024)}, u32[]{:S(2)}) copy-start(f32[7168]{0:T(1024)} %param.11) | copy-start | bytes 86020
  7.2 140.7 %all-gather.3.cloned.1.call-start = ((), (), s32[]{:S(2)}) async-start(), calls=%async_computation.2 | async-start | bytes 14155776 | tf_op jit(solution)/shard_map/all_gather | solution.py:92
  10.7 1.2 copy-start.1
  11.9 1.3 copy-start.11
  13.2 14.0 %copy-start.8 = (f32[3,512]{1,0:T(4,128)S(1)}, f32[3,512]{1,0:T(4,128)}, u32[]{:S(2)}) copy-start(f32[3,512]{1,0:T(4,128)} %param.15) | copy-start | bytes 18436
  13.2 14.0 %copy-start.5 = (s32[1024]{0:T(1024)S(1)}, s32[1024]{0:T(1024)}, u32[]{:S(2)}) copy-start(s32[1024]{0:T(1024)} %param.16) | copy-start | bytes 12292
  16.7 180.7 %all-to-all-start.1 = ((s32[16,4,1]{1,2,0:T(1,128)}), s32[16,4,1]{1,2,0:T(1,128)S(1)}, u32[]{:S(2)}, u32[]{:S(2)}) async-start(s32[16,4,1]{1,2,0:T(1,128)} %bitcast.6), calls=%async_computation.1 | async-start | bytes 16384 | tf_op jit(solution)/shard_map/all_to_all | solution.py:83
  25.2 159.7 %all-gather.5.cloned.1.call-start = ((), (), s32[]{:S(2)}) async-start(), calls=%async_computation.3 | async-start | bytes 2359296 | tf_op jit(solution)/shard_map/all_gather | solution.py:92
  147.9 11.6 %copy-start.9 = (bf16[1024,6144]{1,0:T(8,128)(2,1)S(1)}, bf16[1024,6144]{1,0:T(8,128)(2,1)}, u32[]{:S(2)}) copy-start(bf16[1024,6144]{1,0:T(8,128)(2,1)} %all-gather.3.cloned.1.call-done) | copy-start | bytes 37748740
  147.9 21.6 %slice-start = ((s8[7340032]{0:T(1024)(128)(4,1)}), s8[4194304]{0:T(1024)(128)(4,1)S(1)}, s32[]{:S(2)}) async-start(s8[7340032]{0:T(1024)(128)(4,1)} %bitcast.22), calls=%async_computation.4 | async-start | bytes 8388608
  159.5 10.0 %slice-start.1 = ((s8[7340032]{0:T(1024)(128)(4,1)}), s8[3145728]{0:T(1024)(128)(4,1)S(1)}, s32[]{:S(2)}) async-start(s8[7340032]{0:T(1024)(128)(4,1)} %bitcast.22), calls=%async_computation.5 | async-start | bytes 6291456
  188.0 1.6 copy-start.2
  188.3 2.0 copy-start.10
  193.5 1.0 copy-start.3
  193.8 1.3 copy-start.4
  197.5 41.0 %all-to-all-start = ((bf16[64,2,16,4,128]{4,2,3,1,0:T(8,128)(2,1)}), bf16[64,2,16,4,128]{4,2,3,1,0:T(8,128)(2,1)S(1)}, u32[]{:S(2)}, u32[]{:S(2)}) async-start(bf16[64,2,16,4,128]{4,2,3,1,0:T(8,128)(2,1)} %gather_fusion), calls=%async_computation | async-start | bytes 4194304 | tf_op jit(solution)/shard_map/all_to_all | solution.py:82
Sparse Core Ops, SparseCore 0:
  13.3 134.5 all-gather.2
  150.1 34.7 all-gather.4
